TPU v7x, 32 devices: a whole 2x2x4 slice. The times are simulated.
32 devices in a mesh: dp: 8 (over y, x, core), tensor: 4 (over z).
Axes of the slice: x: 2, y: 2, z: 4, core: 2. Of those that a mesh axis runs over, the one named last changes fastest.
Arguments:
- inputs: bfloat16 [32768, 768], P('dp'), may hold values from -6 to 6
- segments: int32 [64, 512], P('dp'), may hold values from 0 to 7, never falling along the last dimension, each value on 1 to 128 neighbouring positions
- w_query: bfloat16 [768, 768], P(None, 'tensor'), may hold values from -0.21875 to 0.21875
- w_key: bfloat16 [768, 768], P(None, 'tensor'), may hold values from -0.21875 to 0.21875
- w_value: bfloat16 [768, 768], P(None, 'tensor'), may hold values from -0.21875 to 0.21875
- b_query: bfloat16 [768], P('tensor'), may hold values from -3 to 3
- b_value: bfloat16 [768], P('tensor'), may hold values from -3 to 3
- w_output: bfloat16 [768, 768], P('tensor'), may hold values from -0.875 to 0.875
- b_output: bfloat16 [768], replicated, may hold values from -3 to 3
- gain_attn: bfloat16 [768], replicated, may hold values from 0.5 to 1.5
- shift_attn: bfloat16 [768], replicated, may hold values from -3 to 3
- w_hidden: bfloat16 [768, 3072], P(None, 'tensor'), may hold values from -0.21875 to 0.21875
- b_hidden: bfloat16 [3072], P('tensor'), may hold values from -3 to 3
- w_project: bfloat16 [3072, 768], P('tensor'), may hold values from -0.109375 to 0.109375
- b_project: bfloat16 [768], replicated, may hold values from -3 to 3
- gain_ffn: bfloat16 [768], replicated, may hold values from 0.5 to 1.5
- shift_ffn: bfloat16 [768], replicated, may hold values from -3 to 3
- cotangent: bfloat16 [32768, 768], P(('dp', 'tensor')), may hold values from -6 to 6
Outputs:
- output: bfloat16 [32768, 768], P(('dp', 'tensor'))
- grad_input: float32 [32768, 768], P(('dp', 'tensor'))
- grad_w_query: float32 [768, 768], P('dp', 'tensor')
- grad_w_key: float32 [768, 768], P('dp', 'tensor')
- grad_w_value: float32 [768, 768], P('dp', 'tensor')
- grad_w_output: float32 [768, 768], P('tensor', 'dp')
- grad_w_hidden: float32 [768, 3072], P('dp', 'tensor')
- grad_w_project: float32 [3072, 768], P('tensor', 'dp')
- grad_bias_qv: float32 [2, 12, 64], P(None, 'tensor', 'dp')
- grad_b_hidden: float32 [48, 64], P('tensor', 'dp')
- grad_vectors: float32 [6, 768], P(None, ('dp', 'tensor'))
Inputs may be any that keep to these rules, and one draw needn't show every extreme that they name: `segments`: within each row of 512 tokens segment numbers never fall; each text holds 1 to 128 tokens, and some text holds exactly 128.
All inputs are finite; a program needn't handle non-finite values.
Results may differ from a plain program's by a relative error of at most 0.014.
Values may be sent and summed in bfloat16 or wider, within the bound.
A program may use at most 192 MiB of HBM per device.

v0:
```python
import jax
import jax.numpy as jnp
from jax import lax
from jax.sharding import PartitionSpec as P

HD = 64
norm_epsilon = 1e-12
root_half = 0.7071067811865476


def norm_forward(values, norm_gain, norm_shift):
    average = jnp.mean(values, axis=-1, keepdims=True)
    centered = values - average
    variance = jnp.mean(centered * centered, axis=-1, keepdims=True)
    inverse = lax.rsqrt(variance + norm_epsilon)
    scaled = centered * inverse
    return (scaled * norm_gain + norm_shift, scaled, inverse)


def norm_backward(grad_out, scaled, inverse, norm_gain):
    weighted = grad_out * norm_gain
    mean_grad = jnp.mean(weighted, axis=-1, keepdims=True)
    mean_proj = jnp.mean(weighted * scaled, axis=-1, keepdims=True)
    return inverse * (weighted - mean_grad - scaled * mean_proj)


def gelu_exact(values):
    return 0.5 * values * (1.0 + lax.erf(values * root_half))


def cross_rows(left, right):
    return lax.dot_general(
        left, right, (((0,), (0,)), ((), ())), preferred_element_type=jnp.float32
    )


def times_transposed(left, right):
    return lax.dot_general(
        left, right, (((1,), (1,)), ((), ())), preferred_element_type=jnp.float32
    )


def masked_scores(queries, keys_in, segment_row):
    same_text = segment_row[:, None] == segment_row[None, :]
    scores = jnp.einsum("qhd,khd->hqk", queries, keys_in, preferred_element_type=jnp.float32)
    scores = scores * queries.shape[2] ** (-0.5)
    return jnp.where(same_text[None], scores, -1000000000.0)


def attend_forward(packed):
    queries, keys_in, values, segment_row = packed
    scores = masked_scores(queries, keys_in, segment_row)
    row_max = jnp.max(scores, axis=-1, keepdims=True)
    exponent = jnp.exp(scores - row_max)
    row_total = jnp.sum(exponent, axis=-1, keepdims=True)
    attn_probs = (exponent / row_total).astype(jnp.bfloat16)
    mixed_heads = jnp.einsum("hqk,khd->qhd", attn_probs, values, preferred_element_type=jnp.float32)
    return (mixed_heads.astype(jnp.bfloat16), row_max + jnp.log(row_total))


def attend_backward(packed):
    queries, keys_in, values, segment_row, logsum, grad_mixed = packed
    score_scale = queries.shape[2] ** (-0.5)
    scores = masked_scores(queries, keys_in, segment_row)
    attn_probs = jnp.exp(scores - logsum)
    grad_probs = jnp.einsum("qhd,khd->hqk", grad_mixed, values, preferred_element_type=jnp.float32)
    grad_values = jnp.einsum(
        "hqk,qhd->khd",
        attn_probs.astype(jnp.bfloat16),
        grad_mixed,
        preferred_element_type=jnp.float32,
    )
    inner_sum = jnp.sum(attn_probs * grad_probs, axis=-1, keepdims=True)
    grad_scores = (attn_probs * (grad_probs - inner_sum)).astype(jnp.bfloat16)
    grad_queries = (
        jnp.einsum("hqk,khd->qhd", grad_scores, keys_in, preferred_element_type=jnp.float32)
        * score_scale
    )
    grad_keys = (
        jnp.einsum("hqk,qhd->khd", grad_scores, queries, preferred_element_type=jnp.float32)
        * score_scale
    )
    return (
        grad_queries.astype(jnp.bfloat16),
        grad_keys.astype(jnp.bfloat16),
        grad_values.astype(jnp.bfloat16),
    )


def per_device(
    inputs,
    segments,
    w_query,
    w_key,
    w_value,
    b_query,
    b_value,
    w_output,
    b_output,
    gain_attn,
    shift_attn,
    w_hidden,
    b_hidden,
    w_project,
    b_project,
    gain_ffn,
    shift_ffn,
    cotangent,
):
    seq_len = segments.shape[1]
    row_count = segments.shape[0]
    token_count = inputs.shape[0]
    share_rows = cotangent.shape[0]
    offset = lax.axis_index("tensor") * share_rows
    head_width = w_query.shape[1]
    head_shape = (row_count, seq_len, head_width // HD, HD)
    attn_gain = gain_attn.astype(jnp.float32)
    attn_shift = shift_attn.astype(jnp.float32)
    attn_bias = b_output.astype(jnp.float32)
    ffn_gain = gain_ffn.astype(jnp.float32)
    ffn_shift = shift_ffn.astype(jnp.float32)
    ffn_bias = b_project.astype(jnp.float32)
    grad_out = cotangent.astype(jnp.float32)
    queries = (
        jnp.dot(inputs, w_query, preferred_element_type=jnp.float32) + b_query.astype(jnp.float32)
    ).astype(jnp.bfloat16)
    keys_in = jnp.dot(inputs, w_key, preferred_element_type=jnp.float32).astype(jnp.bfloat16)
    values = (
        jnp.dot(inputs, w_value, preferred_element_type=jnp.float32) + b_value.astype(jnp.float32)
    ).astype(jnp.bfloat16)
    query_heads = queries.reshape(head_shape)
    key_heads = keys_in.reshape(head_shape)
    value_heads = values.reshape(head_shape)
    mixed_heads, logsum = lax.map(attend_forward, (query_heads, key_heads, value_heads, segments))
    mixed_flat = mixed_heads.reshape(token_count, head_width)
    picked = mixed_flat
    branch_share = lax.psum_scatter(
        jnp.dot(picked, w_output, preferred_element_type=jnp.float32),
        "tensor",
        scatter_dimension=0,
        tiled=True,
    )
    input_share = lax.dynamic_slice_in_dim(inputs, offset, share_rows, 0).astype(jnp.float32)
    hidden_share = input_share + (branch_share + attn_bias)
    hidden_all = lax.all_gather(hidden_share, "tensor", axis=0, tiled=True)
    normed_all, scaled_all, inverse_all = norm_forward(hidden_all, attn_gain, attn_shift)
    normed_low = normed_all.astype(jnp.bfloat16)
    normed_share = lax.dynamic_slice_in_dim(normed_all, offset, share_rows, 0)
    scaled_share = lax.dynamic_slice_in_dim(scaled_all, offset, share_rows, 0)
    hidden_pre = jnp.dot(
        normed_low, w_hidden, preferred_element_type=jnp.float32
    ) + b_hidden.astype(jnp.float32)
    active, gelu_pull = jax.vjp(gelu_exact, hidden_pre)
    active_low = active.astype(jnp.bfloat16)
    picked = active_low
    second_share = lax.psum_scatter(
        jnp.dot(picked, w_project, preferred_element_type=jnp.float32),
        "tensor",
        scatter_dimension=0,
        tiled=True,
    )
    block_sum = normed_share + (second_share + ffn_bias)
    output_share, scaled_out, inverse_out = norm_forward(block_sum, ffn_gain, ffn_shift)
    grad_sum = norm_backward(grad_out, scaled_out, inverse_out, ffn_gain)
    grad_ffn_gain = jnp.sum(grad_out * scaled_out, axis=0)
    grad_ffn_shift = jnp.sum(grad_out, axis=0)
    grad_sum_low = grad_sum.astype(jnp.bfloat16)
    grad_ffn_bias = jnp.sum(grad_sum_low.astype(jnp.float32), axis=0)
    grad_sum_all = lax.all_gather(grad_sum_low, "tensor", axis=0, tiled=True)
    grad_active = times_transposed(grad_sum_all, w_project)
    grad_w_project = cross_rows(active_low, grad_sum_all)
    grad_hidden_pre = gelu_pull(grad_active)[0].astype(jnp.bfloat16)
    grad_b_hidden = jnp.sum(grad_hidden_pre.astype(jnp.float32), axis=0).reshape(-1, HD)
    grad_w_hidden = cross_rows(normed_low, grad_hidden_pre)
    picked = grad_hidden_pre
    grad_normed_share = grad_sum + lax.psum_scatter(
        times_transposed(picked, w_hidden), "tensor", scatter_dimension=0, tiled=True
    )
    grad_normed_all = lax.all_gather(grad_normed_share, "tensor", axis=0, tiled=True)
    grad_hidden_all = norm_backward(grad_normed_all, scaled_all, inverse_all, attn_gain)
    grad_hidden_share = lax.dynamic_slice_in_dim(grad_hidden_all, offset, share_rows, 0)
    grad_hidden_low = grad_hidden_all.astype(jnp.bfloat16)
    grad_attn_gain = jnp.sum(grad_normed_share * scaled_share, axis=0)
    grad_attn_shift = jnp.sum(grad_normed_share, axis=0)
    grad_attn_bias = jnp.sum(grad_hidden_share.astype(jnp.bfloat16).astype(jnp.float32), axis=0)
    grad_w_output = cross_rows(mixed_flat, grad_hidden_low)
    grad_mixed = (
        times_transposed(grad_hidden_low, w_output).astype(jnp.bfloat16).reshape(head_shape)
    )
    grad_query_heads, grad_key_heads, grad_value_heads = lax.map(
        attend_backward, (query_heads, key_heads, value_heads, segments, logsum, grad_mixed)
    )
    grad_queries = grad_query_heads.reshape(token_count, head_width)
    grad_keys = grad_key_heads.reshape(token_count, head_width)
    grad_values = grad_value_heads.reshape(token_count, head_width)
    grad_w_query = cross_rows(inputs, grad_queries)
    grad_w_key = cross_rows(inputs, grad_keys)
    grad_w_value = cross_rows(inputs, grad_values)
    grad_b_query = jnp.sum(grad_queries.astype(jnp.float32), axis=0)
    grad_b_value = jnp.sum(grad_values.astype(jnp.float32), axis=0)
    grad_bias_qv = jnp.stack([grad_b_query, grad_b_value]).reshape(2, head_width // HD, HD)
    summed = times_transposed(grad_queries, w_query)
    summed = summed + times_transposed(grad_keys, w_key)
    grad_input = grad_hidden_share + lax.psum_scatter(
        (summed + times_transposed(grad_values, w_value)).astype(jnp.bfloat16),
        "tensor",
        scatter_dimension=0,
        tiled=True,
    ).astype(jnp.float32)
    all_parts = (
        lax.psum_scatter(grad_w_query, "dp", scatter_dimension=0, tiled=True),
        lax.psum_scatter(grad_w_key, "dp", scatter_dimension=0, tiled=True),
        lax.psum_scatter(grad_w_value, "dp", scatter_dimension=0, tiled=True),
        lax.psum_scatter(grad_w_output, "dp", scatter_dimension=1, tiled=True),
        lax.psum_scatter(grad_w_hidden, "dp", scatter_dimension=0, tiled=True),
        lax.psum_scatter(grad_w_project, "dp", scatter_dimension=1, tiled=True),
        lax.psum_scatter(grad_bias_qv, "dp", scatter_dimension=2, tiled=True),
        lax.psum_scatter(grad_b_hidden, "dp", scatter_dimension=1, tiled=True),
    )
    (
        sum_query,
        sum_key,
        sum_value,
        sum_output,
        sum_hidden,
        sum_project,
        sum_bias_qv,
        sum_b_hidden,
    ) = all_parts
    vector_stack = jnp.stack(
        [
            grad_attn_gain,
            grad_attn_shift,
            grad_attn_bias,
            grad_ffn_gain,
            grad_ffn_shift,
            grad_ffn_bias,
        ]
    )
    sum_vectors = lax.psum_scatter(vector_stack, ("dp", "tensor"), scatter_dimension=1, tiled=True)
    return (
        output_share.astype(jnp.bfloat16),
        grad_input,
        sum_query,
        sum_key,
        sum_value,
        sum_output,
        sum_hidden,
        sum_project,
        sum_bias_qv,
        sum_b_hidden,
        sum_vectors,
    )


def solution(mesh):
    in_specs = (
        P("dp", None),
        P("dp", None),
        P(None, "tensor"),
        P(None, "tensor"),
        P(None, "tensor"),
        P("tensor"),
        P("tensor"),
        P("tensor", None),
        P(),
        P(),
        P(),
        P(None, "tensor"),
        P("tensor"),
        P("tensor", None),
        P(),
        P(),
        P(),
        P(("dp", "tensor"), None),
    )
    out_specs = (
        P(("dp", "tensor"), None),
        P(("dp", "tensor"), None),
        P("dp", "tensor"),
        P("dp", "tensor"),
        P("dp", "tensor"),
        P("tensor", "dp"),
        P("dp", "tensor"),
        P("tensor", "dp"),
        P(None, "tensor", "dp"),
        P("tensor", "dp"),
        P(None, ("dp", "tensor")),
    )
    return jax.shard_map(
        per_device, mesh=mesh, in_specs=in_specs, out_specs=out_specs, check_vma=False
    )
```

profile of v0, /device:TPU:0, one launch (start us, length us, event | category | flops | bytes accessed | tf_op | source)
XLA Modules:
  0.0 1853.3 jit_solution(15079120562952520668)
XLA Ops:
  26.3 48.8 %while.26 = (s32[]{:T(128)}, bf16[8,512,3,64]{1,3,2,0:T(8,128)(2,1)}, f32[8,3,512,1]{2,1,3,0:T(4,128)S(1)}, bf16[8,512,3,64]{1,3,2,0:T(8,128)(2,1)}, s32[8,512]{...) while((s32[]{:T(128)}, ...), condition=%wide.region_3.4_spmd, body=%wide.region_0.3_spmd.sunk | while | flops 211122688 | bytes 11335781 | solution.py:134
  78.6 6.4 fusion.79
  85.7 214.1 %reduce-scatter.22.cloned.1.call-done = f32[1024,768]{1,0:T(8,128)} async-done(((f32[4096,768]{1,0:T(8,128)}), f32[1024,768]{1,0:T(8,128)}) %reduce-scatter.22.cloned.1.call-update) | async-done | bytes 3145744 | tf_op jit(solution)/shard_map/reduce_scatter | solution.py:137
  304.9 218.7 %all-gather.4.cloned.1.call-done = f32[4096,768]{1,0:T(8,128)} async-done(((f32[1024,768]{1,0:T(8,128)}), f32[4096,768]{1,0:T(8,128)}) %all-gather.4.cloned.1.call-update) | async-done | bytes 12582928 | tf_op jit(solution)/shard_map/all_gather | solution.py:145
  528.8 6.0 multiply_reduce_fusion.2
  534.8 11.5 multiply_add_fusion
  546.3 10.4 multiply_convert_fusion.1
  556.8 10.6 fusion.80
  568.0 209.6 %reduce-scatter.24.cloned.1.call-done = f32[1024,768]{1,0:T(8,128)} async-done(((f32[4096,768]{1,0:T(8,128)}), f32[1024,768]{1,0:T(8,128)}) %reduce-scatter.24.cloned.1.call-update) | async-done | bytes 3145744 | tf_op jit(solution)/shard_map/reduce_scatter | solution.py:156
  788.5 116.4 %all-gather.6.cloned.1.call-done = bf16[4096,768]{1,0:T(8,128)(2,1)} async-done(((bf16[1024,768]{1,0:T(8,128)(2,1)}), bf16[4096,768]{1,0:T(8,128)(2,1)}) %all-gather.6.cloned.1.call-update) | async-done | bytes 6291472 | tf_op jit(solution)/shard_map/all_gather | solution.py:169
  905.0 13.3 convert_reduce_fusion
  920.9 8.3 fusion.81
  929.9 209.5 %reduce-scatter.26.cloned.1.call-done = f32[1024,768]{1,0:T(8,128)} async-done(((f32[4096,768]{1,0:T(8,128)}), f32[1024,768]{1,0:T(8,128)}) %reduce-scatter.26.cloned.1.call-update) | async-done | bytes 3145744 | tf_op jit(solution)/shard_map/reduce_scatter | solution.py:176
  1139.4 6.4 fusion.75
  1145.9 219.3 %all-gather.8.cloned.1.call-done = f32[4096,768]{1,0:T(8,128)} async-done(((f32[1024,768]{1,0:T(8,128)}), f32[4096,768]{1,0:T(8,128)}) %all-gather.8.cloned.1.call-update) | async-done | bytes 12582928 | tf_op jit(solution)/shard_map/all_gather | solution.py:179
  1365.2 9.9 multiply_reduce_fusion.3
  1375.1 9.7 subtract_multiply_fusion
  1392.7 6.8 convolution_convert_fusion
  1404.8 91.0 %while.27 = (s32[]{:T(128)}, bf16[8,512,3,64]{1,3,2,0:T(8,128)(2,1)}, bf16[8,512,3,64]{1,3,2,0:T(8,128)(2,1)}, bf16[8,512,3,64]{1,3,2,0:T(8,128)(2,1)S(1)}, bf16...) while((s32[]{:T(128)}, ...), condition=%wide.region_17.18_spmd, body=%wide.region_15.17_spmd.sunk | while | flops 511146496 | bytes 26125436 | solution.py:190
  1502.3 6.3 fusion.83
  1508.6 6.5 fusion.82
  1515.1 12.8 add_convert_fusion
  1527.9 11.9 fusion.66
  1539.8 10.1 fusion.84
  1571.3 24.6 %all-reduce.3 = (f32[2,3,64]{2,1,0:T(4,128)S(1)}, f32[12,64]{1,0:T(8,128)S(1)}) all-reduce(f32[2,3,64]{2,1,0:T(4,128)S(1)} %pad_maximum_fusion, f32[12,64]{1,0:T(8,128)S(1)} %reshape.201), channel_id=12, replica_groups=mesh['dp'=8,'tensor'=4] {'dp'}, use_global_device_ids=true, to_apply=%region_27.28.clone | all-reduce | flops 1152 | bytes 9216
  1599.0 37.9 %reduce-scatter.28.cloned.1.call-done = bf16[1024,768]{1,0:T(8,128)(2,1)} async-done(((bf16[4096,768]{1,0:T(8,128)(2,1)}), bf16[1024,768]{1,0:T(8,128)(2,1)}) %reduce-scatter.28.cloned.1.call-update) | async-done | bytes 1572880 | tf_op jit(solution)/shard_map/reduce_scatter | solution.py:204
  1636.9 5.4 convert_reduce_fusion.3
  1642.4 41.1 %all-reduce.2 = f32[6,768]{1,0:T(8,128)S(1)} all-reduce(f32[6,768]{1,0:T(8,128)S(1)} %stack.39), channel_id=14, replica_groups=mesh['dp'=8,'tensor'=4] {'dp','tensor'}, use_global_device_ids=true, to_apply=%region_36.37.clone | all-reduce | flops 4608 | bytes 36864
  1684.4 46.0 %reduce-scatter.32.cloned.1.call-done = f32[768,96]{0,1:T(8,128)} async-done(((f32[768,768]{0,1:T(8,128)}), f32[768,96]{0,1:T(8,128)}) %reduce-scatter.32.cloned.1.call-update) | async-done | bytes 294928 | tf_op jit(solution)/shard_map/reduce_scatter | solution.py:216
  1730.4 38.7 %reduce-scatter.34.cloned.1.call-done = f32[96,192]{1,0:T(8,128)} async-done(((f32[768,192]{1,0:T(8,128)}), f32[96,192]{1,0:T(8,128)}) %reduce-scatter.34.cloned.1.call-update) | async-done | bytes 73744
  1769.1 38.5 %reduce-scatter.38.cloned.1.call-done = f32[96,192]{1,0:T(8,128)} async-done(((f32[768,192]{1,0:T(8,128)}), f32[96,192]{1,0:T(8,128)}) %reduce-scatter.38.cloned.1.call-update) | async-done | bytes 73744
  1807.6 38.7 %reduce-scatter.36.cloned.1.call-done = f32[96,192]{1,0:T(8,128)} async-done(((f32[768,192]{1,0:T(8,128)}), f32[96,192]{1,0:T(8,128)}) %reduce-scatter.36.cloned.1.call-update) | async-done | bytes 73744
  (283 shorter events, 231.5 us)
Async XLA Ops:
  7.2 539.1 %copy-start = (bf16[768,768]{1,0:T(8,128)(2,1)S(1)}, bf16[768,768]{1,0:T(8,128)(2,1)}, u32[]{:S(2)}) copy-start(bf16[768,768]{1,0:T(8,128)(2,1)} %param.33) | copy-start | bytes 3538948
  7.2 292.6 %reduce-scatter.22.cloned.1.call-start = ((), (), s32[]{:S(2)}) async-start(), calls=%async_computation.10 | async-start | bytes 15728640 | tf_op jit(solution)/shard_map/reduce_scatter | solution.py:137
  8.6 7.3 copy-start.17
  13.7 3.4 copy-start.13
  75.0 3.5 copy-start.12
  85.1 438.5 %all-gather.4.cloned.1.call-start = ((), (), s32[]{:S(2)}) async-start(), calls=%async_computation.11 | async-start | bytes 15728640 | tf_op jit(solution)/shard_map/all_gather | solution.py:145
  304.2 473.4 %reduce-scatter.24.cloned.1.call-start = ((), (), s32[]{:S(2)}) async-start(), calls=%async_computation.12 | async-start | bytes 15728640 | tf_op jit(solution)/shard_map/reduce_scatter | solution.py:156
  546.3 10.5 copy-start.3
  546.3 10.4 copy-start.30
  567.4 337.6 %all-gather.6.cloned.1.call-start = ((), (), s32[]{:S(2)}) async-start(), calls=%async_computation.13 | async-start | bytes 7864320 | tf_op jit(solution)/shard_map/all_gather | solution.py:169
  780.9 4.9 copy-start.4
  788.5 351.0 %reduce-scatter.26.cloned.1.call-start = ((), (), s32[]{:S(2)}) async-start(), calls=%async_computation.14 | async-start | bytes 15728640 | tf_op jit(solution)/shard_map/reduce_scatter | solution.py:176
  929.2 436.0 %all-gather.8.cloned.1.call-start = ((), (), s32[]{:S(2)}) async-start(), calls=%async_computation.15 | async-start | bytes 15728640 | tf_op jit(solution)/shard_map/all_gather | solution.py:179
  1145.8 451.5 %reduce-scatter.40.cloned.1.call-start = ((), (), s32[]{:S(2)}) async-start(), calls=%async_computation.22 | async-start | bytes 884736
  1384.8 4.5 copy-start.2
  1399.5 237.4 %reduce-scatter.28.cloned.1.call-start = ((), (), s32[]{:S(2)}) async-start(), calls=%async_computation.16 | async-start | bytes 7864320 | tf_op jit(solution)/shard_map/reduce_scatter | solution.py:204
  1498.7 3.5 copy-start.9
  1500.3 14.8 copy-start.11
  1502.2 6.4 copy-start.10
  1502.3 6.3 copy-start.18
  1508.6 6.5 copy-start.14
  1527.9 156.5 %reduce-scatter.30.cloned.1.call-start = ((), (), s32[]{:S(2)}) async-start(), calls=%async_computation.17 | async-start | bytes 2654208 | tf_op jit(solution)/shard_map/reduce_scatter | solution.py:215
  1539.8 190.6 %reduce-scatter.32.cloned.1.call-start = ((), (), s32[]{:S(2)}) async-start(), calls=%async_computation.18 | async-start | bytes 2654208 | tf_op jit(solution)/shard_map/reduce_scatter | solution.py:216
  1550.0 219.1 %reduce-scatter.34.cloned.1.call-start = ((), (), s32[]{:S(2)}) async-start(), calls=%async_computation.19 | async-start | bytes 884736
  1555.9 6.1 copy-start.31
  1555.9 7.3 copy-start.21
  1556.0 7.3 copy-start.20
  1556.0 7.3 copy-start.19
  1556.0 7.3 copy-start.22
  1556.0 251.6 %reduce-scatter.38.cloned.1.call-start = ((), (), s32[]{:S(2)}) async-start(), calls=%async_computation.21 | async-start | bytes 884736
  1561.9 284.3 %reduce-scatter.36.cloned.1.call-start = ((), (), s32[]{:S(2)}) async-start(), calls=%async_computation.20 | async-start | bytes 884736
  1597.3 249.0 %copy-start.1 = (bf16[768,768]{1,0:T(8,128)(2,1)S(1)}, bf16[768,768]{1,0:T(8,128)(2,1)}, u32[]{:S(2)}) copy-start(bf16[768,768]{1,0:T(8,128)(2,1)} %param.33) | copy-start | bytes 3538948
  (13 other events, 17.6 us)
Sparse Core Ops, SparseCore 0:
  85.2 214.6 reduce-scatter.21
  304.3 219.2 all-gather.3
  567.5 210.0 reduce-scatter.23
  788.6 116.3 all-gather.5
  929.3 210.0 reduce-scatter.25
  1145.9 219.2 all-gather.7
  1399.7 33.1 reduce-scatter.39
  1528.0 108.9 reduce-scatter.27
  1640.9 43.4 reduce-scatter.29
  1688.2 42.1 reduce-scatter.31
  1734.1 34.9 reduce-scatter.33
  1772.6 34.9 reduce-scatter.37
  1811.3 34.9 reduce-scatter.35
where the time goes:
time: 1860 us; the launch traced here: 1850 us
  waiting for transfers between devices  1390 us (75%)
  matrix products  242 us (13%)
  other arithmetic  86.3 us (5%)
  blocking collectives  65.7 us (4%)
  local copies, waits for them, and re-layouts  54.6 us (3%)
    all_gather x1, waiting for transfers between devices, per_device(): lax.all_gather(grad_normed_share, 'tensor', axis=0, tiled=True)  219 us
    all_gather x1, waiting for transfers between devices, per_device(): hidden_all = lax.all_gather(hidden_share, 'tensor', axis=0, tiled=True)  219 us
    reduce_scatter x1, waiting for transfers between devices, per_device(): lax.psum_scatter(jnp.dot(picked, w_output, preferred_element_type=jnp.flo...  214 us
    reduce_scatter x1, waiting for transfers between devices, per_device(): lax.psum_scatter(jnp.dot(picked, w_project, preferred_element_type=jnp.fl...  210 us
    reduce_scatter x1, waiting for transfers between devices, per_device(): lax.psum_scatter(times_transposed(picked, w_hidden), 'tensor', scatter_di...  210 us
    all_gather x1, waiting for transfers between devices, per_device(): grad_sum_all = lax.all_gather(grad_sum_low, 'tensor', axis=0, tiled=True)  116 us
    unnamed x17, waiting for transfers between devices  116 us
    unnamed x2, blocking collectives  65.7 us
  transfers between devices with their start and end apart: 13, of which 12 were waited for; matrix products, arithmetic and copies ran while one was open for 10% of the time, Pallas kernels for 0%

commit v1 on v0

--- a/solution.py
+++ b/solution.py
@@ -6,6 +6,28 @@
 HD = 64
 norm_epsilon = 1e-12
 root_half = 0.7071067811865476
+
+
+def joined_along(blocks, dim):
+    shape = list(blocks.shape[1:])
+    shape[dim] *= blocks.shape[0]
+    return jnp.moveaxis(blocks, 0, dim).reshape(shape)
+
+
+def ring_gather(x, axis, dim):
+    peers = lax.axis_size(axis)
+    pairs = [(i, (i + 1) % peers) for i in range(peers)]
+    back = [(b, a) for a, b in pairs]
+    lower, upper = ([], [])
+    for lap in range(peers - 1):
+        if lap % 2 == 0:
+            lower.append(lax.ppermute(lower[-1] if lower else x, axis, pairs))
+        else:
+            upper.append(lax.ppermute(upper[-1] if upper else x, axis, back))
+    pieces = jnp.stack([*lower[::-1], x, *upper])
+    shift = lax.axis_index(axis) - len(lower)
+    pieces = pieces[(jnp.arange(peers) - shift) % peers]
+    return joined_along(pieces, dim)
 
 
 def norm_forward(values, norm_gain, norm_shift):
@@ -142,7 +164,7 @@
     )
     input_share = lax.dynamic_slice_in_dim(inputs, offset, share_rows, 0).astype(jnp.float32)
     hidden_share = input_share + (branch_share + attn_bias)
-    hidden_all = lax.all_gather(hidden_share, "tensor", axis=0, tiled=True)
+    hidden_all = ring_gather(hidden_share, "tensor", 0)
     normed_all, scaled_all, inverse_all = norm_forward(hidden_all, attn_gain, attn_shift)
     normed_low = normed_all.astype(jnp.bfloat16)
     normed_share = lax.dynamic_slice_in_dim(normed_all, offset, share_rows, 0)

time: 1860 us -> 1890 us (1.016)
  waiting for transfers between devices: 1390 us -> 1310 us
  starting transfers between devices: 0.54 us -> 71.2 us
  local copies, waits for them, and re-layouts: 54.6 us -> 75.6 us
    all_gather x1 -> x0, waiting for transfers between devices: 219 us -> none  [per_device(): hidden_all = lax.all_gather(hidden_share, 'tensor', axis=0, tiled=True)]
    ppermute x0 -> x3, waiting for transfers between devices: none -> 136 us  [the longest x2 136 us: ring_gather(): lower.append(lax.ppermute(lower[-1] if lower else x, axis, pairs))]
    ppermute x0 -> x3, starting transfers between devices: none -> 70.6 us  [the longest x2 68.2 us: ring_gather(): lower.append(lax.ppermute(lower[-1] if lower else x, axis, pairs))]
    unnamed x17 -> x16, waiting for transfers between devices: 116 us -> 116 us
  transfers between devices with their start and end apart: 13 -> 15, of which waited for: 12 -> 14; matrix products, arithmetic and copies ran while one was open for 10% -> 10% of each run, Pallas kernels for 0% -> 0%
where the time goes in v1:
time: 1890 us; the launch traced here: 1880 us
  waiting for transfers between devices  1310 us (69%)
  matrix products  243 us (13%)
  other arithmetic  99.1 us (5%)
  local copies, waits for them, and re-layouts  75.6 us (4%)
  starting transfers between devices  71.2 us (4%)
  blocking collectives  65.5 us (3%)
    all_gather x1, waiting for transfers between devices, per_device(): lax.all_gather(grad_normed_share, 'tensor', axis=0, tiled=True)  219 us
    reduce_scatter x1, waiting for transfers between devices, per_device(): lax.psum_scatter(jnp.dot(picked, w_output, preferred_element_type=jnp.flo...  214 us
    reduce_scatter x1, waiting for transfers between devices, per_device(): lax.psum_scatter(jnp.dot(picked, w_project, preferred_element_type=jnp.fl...  211 us
    reduce_scatter x1, waiting for transfers between devices, per_device(): lax.psum_scatter(times_transposed(picked, w_hidden), 'tensor', scatter_di...  210 us
    ppermute x2, waiting for transfers between devices, ring_gather(): lower.append(lax.ppermute(lower[-1] if lower else x, axis, pairs))  136 us
    all_gather x1, waiting for transfers between devices, per_device(): grad_sum_all = lax.all_gather(grad_sum_low, 'tensor', axis=0, tiled=True)  116 us
    unnamed x16, waiting for transfers between devices  116 us
    ppermute x2, starting transfers between devices, ring_gather(): lower.append(lax.ppermute(lower[-1] if lower else x, axis, pairs))  68.2 us
  transfers between devices with their start and end apart: 15, of which 14 were waited for; matrix products, arithmetic and copies ran while one was open for 10% of the time, Pallas kernels for 0%

profile of v1, /device:TPU:0, one launch (start us, length us, event | category | flops | bytes accessed | tf_op | source)
XLA Modules:
  0.0 1877.6 jit_solution(16767544852023325276)
XLA Ops:
  26.3 53.6 %while.26 = (s32[]{:T(128)}, bf16[8,512,3,64]{1,3,2,0:T(8,128)(2,1)}, f32[8,3,512,1]{2,1,3,0:T(4,128)}, bf16[8,512,3,64]{1,3,2,0:T(8,128)(2,1)}, s32[8,512]{1,0:...) while((s32[]{:T(128)}, bf16[8,512,3,64]{1,3,2,0:T(8,128)(2,1)}, ...), condition=%wide.region_3.4_spmd, body=%wide.region_0.3_spmd.sunk | while | flops 211122688 | bytes 11331685 | solution.py:156
  84.5 6.4 fusion.84
  91.7 214.1 %reduce-scatter.22.cloned.1.call-done = f32[1024,768]{1,0:T(8,128)} async-done(((f32[4096,768]{1,0:T(8,128)}), f32[1024,768]{1,0:T(8,128)}) %reduce-scatter.22.cloned.1.call-update) | async-done | bytes 3145744 | tf_op jit(solution)/shard_map/reduce_scatter | solution.py:159
  313.9 69.3 %collective-permute-done = f32[1024,768]{1,0:T(8,128)} collective-permute-done((f32[1024,768]{1,0:T(8,128)}, f32[1024,768]{1,0:T(8,128)}, u32[]{:S(2)}, u32[]{:S(2)}) %collective-permute-start) | collective-permute-done | bytes 3145760 | tf_op jit(solution)/shard_map/ppermute | solution.py:24
  383.3 66.7 %collective-permute-start.1 = (f32[1024,768]{1,0:T(8,128)}, f32[1024,768]{1,0:T(8,128)}, u32[]{:S(2)}, u32[]{:S(2)}) collective-permute-start(f32[1024,768]{1,0:T(8,128)} %collective-permute-done), channel_id=1, source_target_pairs={{0,1},{1,2},{2,3},{3,0},{4,5},{5,6},{6,7},{7,4},{8,9},{9,10},{10,1... | collective-permute-start | bytes 9437192 | tf_op jit(solution)/shard_map/ppermute | solution.py:24
  450.6 66.3 %collective-permute-done.1 = f32[1024,768]{1,0:T(8,128)} collective-permute-done((f32[1024,768]{1,0:T(8,128)}, f32[1024,768]{1,0:T(8,128)}, u32[]{:S(2)}, u32[]{:S(2)}) %collective-permute-start.1) | collective-permute-done | bytes 3145760 | tf_op jit(solution)/shard_map/ppermute | solution.py:24
  516.9 10.5 pad_maximum_fusion
  527.4 10.4 gather_fusion
  551.2 9.2 multiply_add_fusion
  560.4 13.8 multiply_convert_fusion.1
  576.8 8.1 fusion.85
  585.6 210.6 %reduce-scatter.24.cloned.1.call-done = f32[1024,768]{1,0:T(8,128)} async-done(((f32[4096,768]{1,0:T(8,128)}), f32[1024,768]{1,0:T(8,128)}) %reduce-scatter.24.cloned.1.call-update) | async-done | bytes 3145744 | tf_op jit(solution)/shard_map/reduce_scatter | solution.py:178
  807.1 116.4 %all-gather.3.cloned.1.call-done = bf16[4096,768]{1,0:T(8,128)(2,1)} async-done(((bf16[1024,768]{1,0:T(8,128)(2,1)}), bf16[4096,768]{1,0:T(8,128)(2,1)}) %all-gather.3.cloned.1.call-update) | async-done | bytes 6291472 | tf_op jit(solution)/shard_map/all_gather | solution.py:191
  923.5 13.7 convert_reduce_fusion
  939.9 8.3 fusion.86
  948.8 209.6 %reduce-scatter.26.cloned.1.call-done = f32[1024,768]{1,0:T(8,128)} async-done(((f32[4096,768]{1,0:T(8,128)}), f32[1024,768]{1,0:T(8,128)}) %reduce-scatter.26.cloned.1.call-update) | async-done | bytes 3145744 | tf_op jit(solution)/shard_map/reduce_scatter | solution.py:198
  1164.5 219.3 %all-gather.5.cloned.1.call-done = f32[4096,768]{1,0:T(8,128)} async-done(((f32[1024,768]{1,0:T(8,128)}), f32[4096,768]{1,0:T(8,128)}) %all-gather.5.cloned.1.call-update) | async-done | bytes 12582928 | tf_op jit(solution)/shard_map/all_gather | solution.py:201
  1383.8 9.7 multiply_reduce_fusion.3
  1393.5 9.8 subtract_multiply_fusion
  1411.3 6.8 convolution_convert_fusion
  1423.5 96.3 %while.27 = (s32[]{:T(128)}, bf16[8,512,3,64]{1,3,2,0:T(8,128)(2,1)}, bf16[8,512,3,64]{1,3,2,0:T(8,128)(2,1)}, bf16[8,512,3,64]{1,3,2,0:T(8,128)(2,1)S(1)}, bf16...) while((s32[]{:T(128)}, ...), condition=%wide.region_17.18_spmd, body=%wide.region_15.17_spmd.sunk | while | flops 511146496 | bytes 26125436 | solution.py:212
  1532.7 6.5 fusion.87
  1539.1 12.8 add_convert_fusion
  1552.0 11.7 fusion.67
  1563.8 10.1 fusion.89
  1595.2 24.4 %all-reduce.3 = (f32[2,3,64]{2,1,0:T(4,128)S(1)}, f32[12,64]{1,0:T(8,128)S(1)}) all-reduce(f32[2,3,64]{2,1,0:T(4,128)S(1)} %pad_maximum_fusion.1, f32[12,64]{1,0:T(8,128)S(1)} %reshape.274), channel_id=12, replica_groups=mesh['dp'=8,'tensor'=4] {'dp'}, use_global_device_ids=true, to_apply=%region_27.28.clone | all-reduce | flops 1152 | bytes 9216
  1622.7 38.4 %reduce-scatter.28.cloned.1.call-done = bf16[1024,768]{1,0:T(8,128)(2,1)} async-done(((bf16[4096,768]{1,0:T(8,128)(2,1)}), bf16[1024,768]{1,0:T(8,128)(2,1)}) %reduce-scatter.28.cloned.1.call-update) | async-done | bytes 1572880 | tf_op jit(solution)/shard_map/reduce_scatter | solution.py:226
  1666.5 41.1 %all-reduce.2 = f32[6,768]{1,0:T(8,128)S(1)} all-reduce(f32[6,768]{1,0:T(8,128)S(1)} %stack.59), channel_id=14, replica_groups=mesh['dp'=8,'tensor'=4] {'dp','tensor'}, use_global_device_ids=true, to_apply=%region_36.37.clone | all-reduce | flops 4608 | bytes 36864
  1708.5 46.1 %reduce-scatter.32.cloned.1.call-done = f32[768,96]{0,1:T(8,128)} async-done(((f32[768,768]{0,1:T(8,128)}), f32[768,96]{0,1:T(8,128)}) %reduce-scatter.32.cloned.1.call-update) | async-done | bytes 294928 | tf_op jit(solution)/shard_map/reduce_scatter | solution.py:238
  1754.7 38.5 %reduce-scatter.34.cloned.1.call-done = f32[96,192]{1,0:T(8,128)} async-done(((f32[768,192]{1,0:T(8,128)}), f32[96,192]{1,0:T(8,128)}) %reduce-scatter.34.cloned.1.call-update) | async-done | bytes 73744
  1793.2 38.7 %reduce-scatter.38.cloned.1.call-done = f32[96,192]{1,0:T(8,128)} async-done(((f32[768,192]{1,0:T(8,128)}), f32[96,192]{1,0:T(8,128)}) %reduce-scatter.38.cloned.1.call-update) | async-done | bytes 73744
  1831.9 38.6 %reduce-scatter.36.cloned.1.call-done = f32[96,192]{1,0:T(8,128)} async-done(((f32[768,192]{1,0:T(8,128)}), f32[96,192]{1,0:T(8,128)}) %reduce-scatter.36.cloned.1.call-update) | async-done | bytes 73744
  (298 shorter events, 275.1 us)
Async XLA Ops:
  7.2 553.2 %copy-start = (bf16[768,768]{1,0:T(8,128)(2,1)S(1)}, bf16[768,768]{1,0:T(8,128)(2,1)}, u32[]{:S(2)}) copy-start(bf16[768,768]{1,0:T(8,128)(2,1)} %param.33) | copy-start | bytes 3538948
  7.2 298.6 %reduce-scatter.22.cloned.1.call-start = ((), (), s32[]{:S(2)}) async-start(), calls=%async_computation.10 | async-start | bytes 15728640 | tf_op jit(solution)/shard_map/reduce_scatter | solution.py:159
  8.6 7.3 copy-start.19
  91.0 705.2 %reduce-scatter.24.cloned.1.call-start = ((), (), s32[]{:S(2)}) async-start(), calls=%async_computation.11 | async-start | bytes 15728640 | tf_op jit(solution)/shard_map/reduce_scatter | solution.py:178
  91.7 358.3 %copy-start.26 = (bf16[768]{0:T(1024)(128)(2,1)S(1)}, bf16[768]{0:T(1024)(128)(2,1)}, u32[]{:S(2)}) copy-start(bf16[768]{0:T(1024)(128)(2,1)} %param.31) | copy-start | bytes 4612
  91.7 358.3 %copy-start.27 = (bf16[768]{0:T(1024)(128)(2,1)S(1)}, bf16[768]{0:T(1024)(128)(2,1)}, u32[]{:S(2)}) copy-start(bf16[768]{0:T(1024)(128)(2,1)} %param.34) | copy-start | bytes 4612
  91.7 358.3 %copy-start.28 = (bf16[768]{0:T(1024)(128)(2,1)S(1)}, bf16[768]{0:T(1024)(128)(2,1)}, u32[]{:S(2)}) copy-start(bf16[768]{0:T(1024)(128)(2,1)} %param.32) | copy-start | bytes 4612
  310.1 73.1 %collective-permute-start = (f32[1024,768]{1,0:T(8,128)}, f32[1024,768]{1,0:T(8,128)}, u32[]{:S(2)}, u32[]{:S(2)}) collective-permute-start(f32[1024,768]{1,0:T(8,128)} %add_add_fusion.1), channel_id=1, source_target_pairs={{0,1},{1,2},{2,3},{3,0},{4,5},{5,6},{6,7},{7,4},{8,9},{9,10},{10,1... | collective-permute-start | bytes 9437192 | tf_op jit(solution)/shard_map/ppermute | solution.py:24
  311.6 139.0 %collective-permute-start.2 = (f32[1024,768]{1,0:T(8,128)}, f32[1024,768]{1,0:T(8,128)}, u32[]{:S(2)}, u32[]{:S(2)}) collective-permute-start(f32[1024,768]{1,0:T(8,128)} %add_add_fusion.1), channel_id=1, source_target_pairs={{1,0},{2,1},{3,2},{0,3},{5,4},{6,5},{7,6},{4,7},{9,8},{10,9},{11,1... | collective-permute-start | bytes 9437192 | tf_op jit(solution)/shard_map/ppermute | solution.py:26
  383.3 133.6 %collective-permute-start.1 = (f32[1024,768]{1,0:T(8,128)}, f32[1024,768]{1,0:T(8,128)}, u32[]{:S(2)}, u32[]{:S(2)}) collective-permute-start(f32[1024,768]{1,0:T(8,128)} %collective-permute-done), channel_id=1, source_target_pairs={{0,1},{1,2},{2,3},{3,0},{4,5},{5,6},{6,7},{7,4},{8,9},{9,10},{10,1... | collective-permute-start | bytes 9437192 | tf_op jit(solution)/shard_map/ppermute | solution.py:24
  543.0 8.2 copy-start.3
  560.4 16.4 copy-start.32
  584.9 338.6 %all-gather.3.cloned.1.call-start = ((), (), s32[]{:S(2)}) async-start(), calls=%async_computation.12 | async-start | bytes 7864320 | tf_op jit(solution)/shard_map/all_gather | solution.py:191
  807.0 351.4 %reduce-scatter.26.cloned.1.call-start = ((), (), s32[]{:S(2)}) async-start(), calls=%async_computation.13 | async-start | bytes 15728640 | tf_op jit(solution)/shard_map/reduce_scatter | solution.py:198
  948.2 435.6 %all-gather.5.cloned.1.call-start = ((), (), s32[]{:S(2)}) async-start(), calls=%async_computation.14 | async-start | bytes 15728640 | tf_op jit(solution)/shard_map/all_gather | solution.py:201
  1164.4 456.5 %reduce-scatter.40.cloned.1.call-start = ((), (), s32[]{:S(2)}) async-start(), calls=%async_computation.21 | async-start | bytes 884736
  1393.5 14.3 copy-start.7
  1418.1 242.9 %reduce-scatter.28.cloned.1.call-start = ((), (), s32[]{:S(2)}) async-start(), calls=%async_computation.15 | async-start | bytes 7864320 | tf_op jit(solution)/shard_map/reduce_scatter | solution.py:226
  1524.3 14.8 copy-start.13
  1526.3 6.4 copy-start.12
  1526.3 6.3 copy-start.20
  1532.7 6.5 copy-start.16
  1551.9 156.6 %reduce-scatter.30.cloned.1.call-start = ((), (), s32[]{:S(2)}) async-start(), calls=%async_computation.16 | async-start | bytes 2654208 | tf_op jit(solution)/shard_map/reduce_scatter | solution.py:237
  1563.7 191.0 %reduce-scatter.32.cloned.1.call-start = ((), (), s32[]{:S(2)}) async-start(), calls=%async_computation.17 | async-start | bytes 2654208 | tf_op jit(solution)/shard_map/reduce_scatter | solution.py:238
  1573.9 219.3 %reduce-scatter.34.cloned.1.call-start = ((), (), s32[]{:S(2)}) async-start(), calls=%async_computation.18 | async-start | bytes 884736
  1579.8 7.3 copy-start.23
  1579.8 7.3 copy-start.22
  1579.9 7.3 copy-start.21
  1579.9 7.3 copy-start.24
  1579.9 252.0 %reduce-scatter.38.cloned.1.call-start = ((), (), s32[]{:S(2)}) async-start(), calls=%async_computation.20 | async-start | bytes 884736
  1585.8 284.7 %reduce-scatter.36.cloned.1.call-start = ((), (), s32[]{:S(2)}) async-start(), calls=%async_computation.19 | async-start | bytes 884736
  1620.9 249.5 %copy-start.1 = (bf16[768,768]{1,0:T(8,128)(2,1)S(1)}, bf16[768,768]{1,0:T(8,128)(2,1)}, u32[]{:S(2)}) copy-start(bf16[768,768]{1,0:T(8,128)(2,1)} %param.33) | copy-start | bytes 3538948
  (18 other events, 46.8 us)
Sparse Core Ops, SparseCore 0:
  91.1 214.6 reduce-scatter.21
  585.1 211.0 reduce-scatter.23
  807.1 116.3 all-gather.2
  948.3 210.0 reduce-scatter.25
  1164.6 219.1 all-gather.4
  1418.2 33.0 reduce-scatter.39
  1552.0 108.9 reduce-scatter.27
  1665.0 43.5 reduce-scatter.29
  1712.5 42.1 reduce-scatter.31
  1758.2 34.9 reduce-scatter.33
  1796.9 34.9 reduce-scatter.37
  1835.5 34.9 reduce-scatter.35
